TPU v7x, 128 devices: a whole 4x4x4 slice. The times are simulated.
128 devices in a mesh: row: 8 (over z, core), col: 16 (over x, y).
Axes of the slice: x: 4, y: 4, z: 4, core: 2. Of those that a mesh axis runs over, the one named last changes fastest.
Arguments:
- velocity: float32 [2, 512, 128, 384], P(None, 'col', 'row'), may hold values from -6 to 6
- synthesis: float32 [384, 384], replicated
- analysis: float32 [384, 384], replicated
- radial_eigen: float32 [384], replicated, may hold values from 0.05 to 4
- pair_list: int32 [256, 2], replicated, may hold values from 0 to 511, as said below
- owner_slot: int32 [256], replicated, may hold values from 0 to 255, each once
- freq_list: int32 [4], replicated, may hold values from 0 to 255
- snap_index: int32 [1], replicated, may hold values from 0 to 254
- block_dft: float32 [256, 4, 2, 384], P(('row', 'col')), may hold values from -6 to 6
- spectra: float32 [256, 4, 2, 384, 384], P(('row', 'col')), may hold values from -6 to 6
Outputs:
- velocity_next: float32 [2, 512, 128, 384], P(None, 'col', 'row')
- block_sums: float32 [256, 4, 2, 384], P(('row', 'col'))
- spectra_next: float32 [256, 4, 2, 384, 384], P(('row', 'col'))
Inputs may be any that keep to these rules, and one draw needn't show every extreme that they name: `pair_list`: the pairs are distinct; the axial index is below 128 and the wavenumber below 512. Of the devices of the solver layout (row index times the size of col plus col index, holding axial indices row * 16 onward and wavenumbers col * 512 / size of col onward), each holds at most 8 selected pairs and some hold exactly 8. `owner_slot`: each slot once.
All inputs are finite; a program needn't handle non-finite values.
Results may differ from a plain program's by a relative error of at most 0.0001.
Values sent between devices are 32-bit elements; how exact they have to be, the bound alone decides.
No kernel may reach another device: no remote copies, remote signals or barrier semaphores. Data moves between devices by JAX's collectives and lax.ppermute only.
A program may use at most 128 MiB of HBM per device.

v0:
```python
import math
import jax
import jax.numpy as jnp
from jax import lax
from jax.sharding import PartitionSpec as P

NBLK = 256
HOLD = 8
viscosity = 4e-06
axial_scale = 2.0
nonlinear_gain = 0.1
highest = lax.Precision.HIGHEST


def sent_together(arrays, axis, split_dim, concat_dim, along):
    both = jnp.concatenate(arrays, axis=along)
    whole, at, outs = (
        lax.all_to_all(both, axis, split_axis=split_dim, concat_axis=concat_dim, tiled=True),
        0,
        [],
    )
    for a in arrays:
        outs.append(lax.slice_in_dim(whole, at, at + a.shape[along], axis=along))
        at += a.shape[along]
    return tuple(outs)


def circle_tables(mode_count, point_count):
    mode_ids = jnp.arange(mode_count, dtype=jnp.int32)[:, None]
    point_ids = jnp.arange(point_count, dtype=jnp.int32)[None, :]
    angle = (mode_ids * point_ids % point_count).astype(jnp.float32) * (2.0 * math.pi / point_count)
    cosine = jnp.cos(angle)
    sine = jnp.sin(angle)
    weight = jnp.where(mode_ids == 0, 1.0, 2.0) * mode_count ** (-0.5)
    keeping = jnp.where(mode_ids == 0, 0.0, math.sqrt(mode_count) / point_count)
    synth_table = jnp.concatenate([weight * cosine, -weight * sine], axis=0)
    anal_table = jnp.concatenate([keeping * cosine, -keeping * sine], axis=0)
    return (synth_table, anal_table)


def circle_forcing(moved, synth_table, anal_table):
    columns = moved.reshape(synth_table.shape[0], -1)
    physical = lax.dot_general(synth_table, columns, (((0,), (0,)), ((), ())), precision=highest)
    squared = physical * physical
    return jnp.dot(anal_table, squared, precision=highest).reshape(moved.shape)


def damping_for(axial_int, mode_int, radial_eigen):
    axial_ids = axial_int.astype(jnp.float32) * axial_scale
    mode_ids = mode_int.astype(jnp.float32)
    return 1.0 / (
        1.0
        + viscosity * (axial_ids[None, :, None] ** 2 + mode_ids[:, None, None] ** 2)
        + radial_eigen[None, None, :]
    )


def radial_apply(rhs, analysis, synthesis, damping):
    radial_pts = rhs.shape[-1]
    coeffs = (
        jnp.dot(rhs.reshape(-1, radial_pts), analysis, precision=highest).reshape(rhs.shape)
        * damping[None]
    )
    return jnp.dot(coeffs.reshape(-1, radial_pts), synthesis, precision=highest).reshape(rhs.shape)


def window_terms(freq_list, snap_now):
    position = snap_now.astype(jnp.float32)
    window = 0.54 - 0.46 * jnp.cos(2.0 * math.pi * position / NBLK)
    phase = (freq_list * snap_now % NBLK).astype(jnp.float32) * (2.0 * math.pi / NBLK)
    return (window * jnp.cos(phase), -window * jnp.sin(phase))


def add_snapshot(block, snapshot, real_w, imag_w):
    real_new = (
        block[:, :, 0]
        + real_w[None, :, None] * snapshot[0][:, None, :]
        - imag_w[None, :, None] * snapshot[1][:, None, :]
    )
    imag_new = (
        block[:, :, 1]
        + real_w[None, :, None] * snapshot[1][:, None, :]
        + imag_w[None, :, None] * snapshot[0][:, None, :]
    )
    return jnp.stack([real_new, imag_new], axis=2)


def spectral_update(spectrum_one, old_block, new_block):
    old_real, old_imag = (old_block[:, 0], old_block[:, 1])
    new_real, new_imag = (new_block[:, 0], new_block[:, 1])
    left_real = jnp.stack([new_real, new_imag, old_real, old_imag], axis=1)
    left_imag = jnp.stack([new_imag, -new_real, old_imag, -old_real], axis=1)
    left = jnp.stack([left_real, left_imag], axis=1)
    right = jnp.stack([new_real, new_imag, -old_real, -old_imag], axis=1)
    return spectrum_one + jnp.einsum("fckr,fkq->fcrq", left, right, precision=highest)


def local(
    velocity,
    synthesis,
    analysis,
    radial_eigen,
    pair_list,
    owner_slot,
    freq_list,
    snap_index,
    block_dft,
    spectra,
):
    modes_dev = velocity.shape[1]
    axial_dev = velocity.shape[2]
    col_count = lax.axis_size("col")
    modes_all = modes_dev * col_count
    synth_table, anal_table = circle_tables(modes_all, 3 * modes_all)
    row_index = lax.axis_index("row")
    col_index = lax.axis_index("col")
    axial_int = row_index * axial_dev + jnp.arange(axial_dev, dtype=jnp.int32)
    mode_int = col_index * modes_dev + jnp.arange(modes_dev, dtype=jnp.int32)
    share = axial_dev // col_count
    state = lax.all_to_all(velocity, "col", split_axis=2, concat_axis=1, tiled=True)
    local_axial = row_index * axial_dev + col_index * share + jnp.arange(share, dtype=jnp.int32)
    local_damping = damping_for(local_axial, jnp.arange(modes_all, dtype=jnp.int32), radial_eigen)
    stepped = []
    for section_index in range(2):
        rhs = state - nonlinear_gain * circle_forcing(state, synth_table, anal_table)
        state = radial_apply(rhs, analysis, synthesis, local_damping)
        stepped.append(state)
    first, second = sent_together((stepped[0], stepped[1]), "col", 1, 2, 0)
    snapshots = [first, second]
    current = snapshots[1]
    selected = pair_list.shape[0]
    slot_ids = jnp.arange(selected, dtype=jnp.int32)
    pair_of_slot = jnp.zeros((selected,), jnp.int32).at[owner_slot].set(slot_ids)
    axial_sel = pair_list[pair_of_slot, 0]
    mode_sel = pair_list[pair_of_slot, 1]
    holder = axial_sel // axial_dev * col_count + mode_sel // modes_dev
    my_index = row_index * col_count + col_index
    both_snaps = jnp.stack(snapshots, axis=0)
    picked = both_snaps[:, :, mode_sel % modes_dev, axial_sel % axial_dev, :]
    slots_here = block_dft.shape[0]
    same_holder = holder[:, None] == holder[None, :]
    earlier = slot_ids[:, None] > slot_ids[None, :]
    position = jnp.sum(jnp.where(same_holder & earlier, 1, 0), axis=1).astype(jnp.int32)
    held_mask = holder == my_index
    hold_slots = HOLD
    placing = jnp.where(
        held_mask[None, :]
        & (position[None, :] == jnp.arange(hold_slots, dtype=jnp.int32)[:, None]),
        1.0,
        0.0,
    )
    compact = jnp.einsum("ps,abst->abpt", placing, picked, precision=highest)
    gathered = lax.all_gather(compact, ("row", "col"), axis=2, tiled=True)
    wanted = my_index * slots_here + jnp.arange(slots_here, dtype=jnp.int32)
    source = holder[wanted] * hold_slots + position[wanted]
    mine = jnp.take(gathered, source, axis=2)
    block = block_dft
    for section_index in range(2):
        real_w, imag_w = window_terms(freq_list, snap_index[0] + section_index)
        block = add_snapshot(block, mine[section_index], real_w, imag_w)
    spectra_next = jax.vmap(spectral_update)(spectra, block_dft, block)
    return (current, block, spectra_next)


def solution(mesh):
    return jax.shard_map(
        local,
        mesh=mesh,
        in_specs=(
            P(None, "col", "row", None),
            P(),
            P(),
            P(),
            P(),
            P(),
            P(),
            P(),
            P(("row", "col"), None, None, None),
            P(("row", "col"), None, None, None, None),
        ),
        out_specs=(
            P(None, "col", "row", None),
            P(("row", "col"), None, None, None),
            P(("row", "col"), None, None, None, None),
        ),
        check_vma=False,
    )
```

profile of v0, /device:TPU:1, one launch (start us, length us, event | category | flops | bytes accessed | tf_op | source)
XLA Modules:
  0.0 276.6 jit_solution(14870041637013253507)
XLA Ops:
  7.2 0.0 copy-start
  7.2 0.0 copy-start.10
  7.2 3.1 %copy.47 = f32[2,32,16,384]{3,1,0,2:T(8,128)} copy(f32[2,32,16,384]{3,2,1,0:T(8,128)} %param.10) | data formatting | bytes 3145728 | tf_op args[0]
  10.3 7.6 %all-to-all-start = ((f32[2,32,16,384]{3,1,0,2:T(8,128)}), f32[2,32,16,384]{3,1,0,2:T(8,128)S(1)}, u32[]{:S(2)}, u32[]{:S(2)}) async-start(f32[2,32,16,384]{3,1,0,2:T(8,128)} %copy.47), calls=%async_computation | async-start | bytes 3145728 | tf_op jit(solution)/shard_map/all_to_all | solution.py:120
  17.9 0.0 copy-done.10
  18.0 0.2 add_divide_fusion
  18.2 14.2 %fusion.12 = (f32[512,1536]{1,0:T(8,128)}, f32[512,1536]{1,0:T(8,128)}) fusion(f32[512]{0:T(512)S(1)} %select_multiply_fusion, f32[512]{0:T(512)S(1)} %fusion.55), kind=kLoop, calls=%fused_computation.27 | loop fusion | flops 8650752 | bytes 6295552 | tf_op jit(solution)/shard_map/mul | solution.py:36
  32.4 14.7 %fusion.13 = (f32[512,1536]{1,0:T(8,128)}, f32[512,1536]{1,0:T(8,128)}) fusion(f32[512]{0:T(512)S(1)} %fusion.43, f32[512]{0:T(512)S(1)} %fusion.54), kind=kLoop, calls=%fused_computation.28 | loop fusion | flops 8650752 | bytes 6295552 | tf_op jit(solution)/shard_map/mul | solution.py:37
  47.1 0.0 all-to-all-done
  47.1 0.0 copy-start.6
  47.1 0.1 copy.48
  47.2 1.8 copy-done.6
  49.0 0.0 copy-start.3
  49.0 12.0 %fusion.4 = f32[1536,384]{1,0:T(8,128)S(1)} fusion(f32[1024,384]{1,0:T(8,128)S(1)} %bitcast.85, f32[512,1536]{1,0:T(8,128)} %get-tuple-element.48, f32[512,1536]{1,0:T(8,128)S(1)} %copy-done.6), kind=kOutput, calls=%fused_computation.15 | convolution fusion | flops 7249920000 | bytes 10223616 | tf_op jit(solution)/shard_map/dot_general | solution.py:43
  61.0 0.0 copy-done.3
  61.0 0.0 copy-done.4
  61.0 10.1 %multiply_subtract_fusion.1 = f32[1024,384]{1,0:T(8,128)S(1)} fusion(f32[1024,384]{1,0:T(8,128)S(1)} %bitcast.86, f32[1536,384]{1,0:T(8,128)S(1)} %fusion.4, f32[512,1536]{1,0:T(8,128)S(1)} %copy-done.4, f32[512,1536]{1,0:T(8,128)S(1)} %copy-done.3), kind=kOutput, calls=%fused_computation.38 | convolution fusion | flops 7250116608 | bytes 11796480 | tf_op jit(solution)/shard_map/dot_general | solution.py:45
  71.1 0.0 copy-start.8
  71.1 0.0 copy-done
  71.1 0.0 copy-start.7
  71.2 3.2 %convolution_multiply_fusion = f32[2,512,384]{2,1,0:T(8,128)S(1)} fusion(f32[2,512,384]{2,1,0:T(8,128)S(1)} %bitcast.87, f32[512,384]{1,0:T(8,128)S(1)} %add_divide_fusion, f32[384,384]{1,0:T(8,128)S(1)} %copy-done), kind=kOutput, calls=%fused_computation.40 | convolution fusion | flops 1812332544 | bytes 4521984 | tf_op jit(solution)/shard_map/dot_general | solution.py:61
  74.4 0.0 copy-done.8
  74.4 3.2 %fusion.77 = f32[1024,384]{1,0:T(8,128)S(1)} fusion(f32[1024,384]{1,0:T(8,128)S(1)} %bitcast.83, f32[384,384]{1,0:T(8,128)S(1)} %copy-done.8), kind=kOutput, calls=%fused_computation.149 | convolution fusion | flops 1811939328 | bytes 3735552 | tf_op jit(solution)/shard_map/dot_general | solution.py:64
  77.6 0.0 copy-done.7
  77.6 10.0 %fusion.5 = f32[1536,384]{1,0:T(8,128)S(1)} fusion(f32[1024,384]{1,0:T(8,128)S(1)} %fusion.77, f32[512,1536]{1,0:T(8,128)S(1)} %copy-done.7, f32[512,1536]{1,0:T(8,128)S(1)} %copy-done.6), kind=kOutput, calls=%fused_computation.16 | convolution fusion | flops 7249920000 | bytes 10223616 | tf_op jit(solution)/shard_map/dot_general | solution.py:43
  87.6 10.4 %multiply_subtract_fusion = f32[1024,384]{1,0:T(8,128)S(1)} fusion(f32[1024,384]{1,0:T(8,128)S(1)} %fusion.77, f32[1536,384]{1,0:T(8,128)S(1)} %fusion.5, f32[512,1536]{1,0:T(8,128)S(1)} %copy-done.4, f32[512,1536]{1,0:T(8,128)S(1)} %copy-done.3), kind=kOutput, calls=%fused_computation.37 | convolution fusion | flops 7250116608 | bytes 11796480 | tf_op jit(solution)/shard_map/dot_general | solution.py:45
  98.0 3.2 %fusion.29 = f32[2,512,384]{2,1,0:T(8,128)S(1)} fusion(f32[2,512,384]{2,1,0:T(8,128)S(1)} %bitcast.84, f32[384,384]{1,0:T(8,128)S(1)} %copy-done), kind=kOutput, calls=%fused_computation.47 | convolution fusion | flops 1811939328 | bytes 3735552 | tf_op jit(solution)/shard_map/dot_general | solution.py:61
  101.2 3.2 %fusion.21 = f32[2,512,1,384]{3,1,0,2:T(8,128)S(1)} fusion(f32[2,512,384]{2,1,0:T(8,128)S(1)} %fusion.29, f32[512,384]{1,0:T(8,128)S(1)} %add_divide_fusion, f32[384,384]{1,0:T(8,128)S(1)} %copy-done.8), kind=kOutput, calls=%fused_computation.39 | convolution fusion | flops 1812332544 | bytes 4521984 | tf_op jit(solution)/shard_map/dot_general | solution.py:64
  104.4 0.2 pad_maximum_fusion.10
  104.7 3.7 %copy.49 = f32[4,512,1,384]{3,0,2,1:T(4,128)} copy(f32[4,512,1,384]{3,1,0,2:T(8,128)S(1)} %pad_maximum_fusion.10) | data formatting | bytes 6291456 | tf_op jit(solution)/shard_map/concatenate | solution.py:16
  108.3 6.8 %all-to-all-start.1 = ((f32[4,512,1,384]{3,0,2,1:T(4,128)}), f32[4,512,1,384]{3,0,2,1:T(4,128)S(1)}, u32[]{:S(2)}, u32[]{:S(2)}) async-start(f32[4,512,1,384]{3,0,2,1:T(4,128)} %copy.49), calls=%async_computation.1 | async-start | bytes 6291456 | tf_op jit(solution)/shard_map/all_to_all | solution.py:18
  115.1 0.0 all-gather.2.cloned.1.call-start
  115.2 0.0 copy-done.11
  115.2 1.4 scatter_custom_fusion
  116.6 0.0 copy-done.2
  116.6 2.5 gather_fusion.1
  119.1 2.5 gather_fusion
  121.6 0.2 select_reduce_fusion
  121.8 33.5 %all-to-all-done.1 = f32[4,512,1,384]{3,0,2,1:T(4,128)S(1)} async-done(((f32[4,512,1,384]{3,0,2,1:T(4,128)}), f32[4,512,1,384]{3,0,2,1:T(4,128)S(1)}, u32[]{:S(2)}, u32[]{:S(2)}) %all-to-all-start.1) | async-done | bytes 3145760 | tf_op jit(solution)/shard_map/all_to_all | solution.py:18
  155.4 0.9 copy.84
  156.2 2.9 %slice_bitcast_fusion = (f32[1,2,32,16,384]{4,1,3,2,0:T(2,128)S(1)}, f32[1,2,32,16,384]{4,1,3,2,0:T(2,128)S(1)}, f32[2,32,16,384]{3,0,2,1:T(2,128)}) fusion(f32[4,32,16,1,384]{4,0,2,1,3:T(4,128)S(1)} %bitcast.80), kind=kLoop, calls=%fused_computation.32 | loop fusion | bytes 7864320 | tf_op jit(solution)/shard_map/stack | solution.py:138
  159.1 1.6 pad_maximum_fusion.11
  160.8 0.0 copy-start.9
  160.8 0.0 copy-start.12
  160.8 3.7 %gather_fusion.4 = f32[256,2,2,384]{3,2,1,0:T(2,128)} fusion(f32[2,2,32,16,384]{4,1,3,2,0:T(2,128)S(1)} %pad_maximum_fusion.11, s32[256]{0:T(256)S(1)} %bitcast.77), kind=kCustom, calls=%fused_computation.4 | custom fusion | bytes 3147776 | tf_op jit(solution)/shard_map/gather | solution.py:139
  164.5 3.1 %fusion.24 = f32[2,2,8,384]{3,2,1,0:T(8,128)} fusion(f32[2,2,256,384]{3,1,0,2:T(2,128)} %bitcast.82, s32[256]{0:T(256)S(1)} %select_reduce_fusion, pred[256]{0:T(512)(128)(4,1)S(1)} %get-tuple-element.24), kind=kOutput, calls=%fused_computation.43 | convolution fusion | flops 37754880 | bytes 1623296 | tf_op jit(solution)/shard_map/ps,abst->abpt/dot_general | solution.py:152
  167.6 0.0 all-gather.2.cloned.1.call-update
  167.7 0.6 gather_fusion.3
  168.3 0.6 gather_fusion.2
  169.8 0.0 copy-done.9
  169.8 0.0 copy-done.12
  169.8 0.1 cosine_multiply_fusion.1
  169.9 0.1 sine_multiply_fusion
  170.0 0.0 copy-done.5
  170.0 1.3 copy.59
  171.2 69.5 %all-gather.2.cloned.1.call-done = f32[2,2,1024,384]{3,2,1,0:T(8,128)} async-done(((f32[2,2,8,384]{3,2,1,0:T(8,128)}), f32[2,2,1024,384]{3,2,1,0:T(8,128)}) %all-gather.2.cloned.1.call-update) | async-done | bytes 6291472 | tf_op jit(solution)/shard_map/all_gather | solution.py:153
  240.7 10.5 %copy.54 = f32[2,2,1024,384]{3,1,2,0:T(2,128)} copy(f32[2,2,1024,384]{3,2,1,0:T(8,128)} %all-gather.2.cloned.1.call-done) | data formatting | bytes 12582912 | tf_op jit(solution)/shard_map/all_gather | solution.py:153
  251.3 3.4 %gather_fusion.5 = f32[2,2,2,384]{3,2,1,0:T(2,128)S(1)} fusion(f32[2,2,1024,384]{3,1,2,0:T(2,128)} %copy.54, s32[1024]{0:T(1024)S(1)} %pad_clamp_fusion), kind=kCustom, calls=%fused_computation.5 | custom fusion | bytes 24584 | tf_op jit(solution)/shard_map/jit(_take)/gather | solution.py:156
  254.6 0.1 select_bitcast_fusion
  254.8 0.1 slice_negate_fusion.1
  254.9 0.6 copy.60
  255.6 0.0 copy-start.1
  255.6 14.0 %convolution_add_fusion = f32[2,4,2,384,384]{4,3,2,1,0:T(8,128)} fusion(f32[2,4,2,384,384]{4,3,2,1,0:T(8,128)} %param.19, f32[2,4,2,4,384]{4,1,3,0,2:T(4,128)S(1)} %pad_maximum_fusion.16, f32[2,4,4,384,1]{3,1,2,0,4:T(4,128)S(1)} %get-tuple-element.30), kind=kOutput, calls=%fused_computation.14 | convolution fusion | flops 115605504 | bytes 19021824 | tf_op jit(solution)/shard_map/vmap(fckr,fkq->fcrq)/dot_general | solution.py:95
  269.6 0.0 copy-done.1
  (28 shorter events, 0.2 us)
Async XLA Ops:
  7.2 64.0 %copy-start = (f32[384,384]{1,0:T(8,128)S(1)}, f32[384,384]{1,0:T(8,128)}, u32[]{:S(2)}) copy-start(f32[384,384]{1,0:T(8,128)} %param.12) | copy-start | bytes 1769476
  7.2 10.8 %copy-start.10 = (f32[384]{0:T(512)S(1)}, f32[384]{0:T(512)}, u32[]{:S(2)}) copy-start(f32[384]{0:T(512)} %param.13) | copy-start | bytes 4612
  10.3 36.8 %all-to-all-start = ((f32[2,32,16,384]{3,1,0,2:T(8,128)}), f32[2,32,16,384]{3,1,0,2:T(8,128)S(1)}, u32[]{:S(2)}, u32[]{:S(2)}) async-start(f32[2,32,16,384]{3,1,0,2:T(8,128)} %copy.47), calls=%async_computation | async-start | bytes 3145728 | tf_op jit(solution)/shard_map/all_to_all | solution.py:120
  47.1 1.9 copy-start.6
  49.0 12.0 %copy-start.3 = (f32[512,1536]{1,0:T(8,128)S(1)}, f32[512,1536]{1,0:T(8,128)}, u32[]{:S(2)}) copy-start(f32[512,1536]{1,0:T(8,128)} %get-tuple-element.49) | copy-start | bytes 9437188
  49.0 12.0 %copy-start.4 = (f32[512,1536]{1,0:T(8,128)S(1)}, f32[512,1536]{1,0:T(8,128)}, u32[]{:S(2)}) copy-start(f32[512,1536]{1,0:T(8,128)} %get-tuple-element.50) | copy-start | bytes 9437188
  71.1 3.2 %copy-start.8 = (f32[384,384]{1,0:T(8,128)S(1)}, f32[384,384]{1,0:T(8,128)}, u32[]{:S(2)}) copy-start(f32[384,384]{1,0:T(8,128)} %param.11) | copy-start | bytes 1769476
  71.1 6.5 %copy-start.7 = (f32[512,1536]{1,0:T(8,128)S(1)}, f32[512,1536]{1,0:T(8,128)}, u32[]{:S(2)}) copy-start(f32[512,1536]{1,0:T(8,128)} %get-tuple-element.48) | copy-start | bytes 9437188
  108.3 6.8 %copy-start.11 = (s32[256]{0:T(256)S(1)}, s32[256]{0:T(256)}, u32[]{:S(2)}) copy-start(s32[256]{0:T(256)} %param.15) | copy-start | bytes 3076
  108.3 8.3 %copy-start.2 = (s32[256,2]{0,1:T(2,128)S(1)}, s32[256,2]{0,1:T(2,128)}, u32[]{:S(2)}) copy-start(s32[256,2]{0,1:T(2,128)} %param.14) | copy-start | bytes 6148
  108.3 47.0 %all-to-all-start.1 = ((f32[4,512,1,384]{3,0,2,1:T(4,128)}), f32[4,512,1,384]{3,0,2,1:T(4,128)S(1)}, u32[]{:S(2)}, u32[]{:S(2)}) async-start(f32[4,512,1,384]{3,0,2,1:T(4,128)} %copy.49), calls=%async_computation.1 | async-start | bytes 6291456 | tf_op jit(solution)/shard_map/all_to_all | solution.py:18
  115.1 125.6 %all-gather.2.cloned.1.call-start = ((), (), s32[]{:S(2)}) async-start(), calls=%async_computation.2 | async-start | bytes 6340608 | tf_op jit(solution)/shard_map/all_gather | solution.py:153
  160.8 9.0 %copy-start.9 = (f32[2,4,2,384]{3,2,1,0:T(2,128)S(1)}, f32[2,4,2,384]{3,2,1,0:T(2,128)}, u32[]{:S(2)}) copy-start(f32[2,4,2,384]{3,2,1,0:T(2,128)} %param.18) | copy-start | bytes 73732
  160.8 9.0 %copy-start.12 = (s32[4]{0:T(128)S(1)}, s32[4]{0:T(128)}, u32[]{:S(2)}) copy-start(s32[4]{0:T(128)} %param.16) | copy-start | bytes 52
  164.5 5.4 %copy-start.5 = (f32[2,32,16,384]{3,0,2,1:T(2,128)S(1)}, f32[2,32,16,384]{3,0,2,1:T(2,128)}, u32[]{:S(2)}) copy-start(f32[2,32,16,384]{3,0,2,1:T(2,128)} %get-tuple-element.28) | copy-start | bytes 4718596
  255.6 14.0 %copy-start.1 = (f32[384,384]{1,0:T(8,128)S(1)}, f32[384,384]{1,0:T(8,128)}, u32[]{:S(2)}) copy-start(f32[384,384]{1,0:T(8,128)} %param.12) | copy-start | bytes 1769476
Sparse Core Ops, SparseCore 0:
  167.8 72.9 all-gather.1
where the time goes:
time: 280 us; the launch traced here: 277 us
  waiting for transfers between devices  103 us (37%)
  matrix products  72.4 us (26%)
  local copies, waits for them, and re-layouts  39.7 us (14%)
  other arithmetic  31.6 us (11%)
  between operations  15.6 us (6%)
  starting transfers between devices  14.4 us (5%)
    all_gather x1, waiting for transfers between devices, local(): gathered = lax.all_gather(compact, ('row', 'col'), axis=2, tiled=True)  69.5 us
    all_to_all x1, waiting for transfers between devices, sent_together(): lax.all_to_all(both, axis, split_axis=split_dim, concat_axis=concat_dim,...  33.5 us
    dot_general x2, matrix products, circle_forcing(): lax.dot_general(synth_table, columns, (((0,), (0,)), ((), ())), precision...  22 us
    dot_general x2, matrix products, circle_forcing(): return jnp.dot(anal_table, squared, precision=highest).reshape(moved.shape)  20.5 us
    mul x1, other arithmetic, circle_tables(): anal_table = jnp.concatenate([keeping * cosine, -keeping * sine], axis=0)  14.7 us
    mul x1, other arithmetic, circle_tables(): synth_table = jnp.concatenate([weight * cosine, -weight * sine], axis=0)  14.2 us
    dot_general x1, matrix products, spectral_update(): jnp.einsum('fckr,fkq->fcrq', left, right, precision=highest)  14 us
    all_gather x1, local copies, waits for them, and re-layouts, local(): gathered = lax.all_gather(compact, ('row', 'col'), axis=2, tiled=True)  10.5 us
  transfers between devices with their start and end apart: 3, of which 2 were waited for; matrix products, arithmetic and copies ran while one was open for 14% of the time, Pallas kernels for 0%

commit v1 on v0

--- a/solution.py
+++ b/solution.py
@@ -150,7 +150,10 @@
         0.0,
     )
     compact = jnp.einsum("ps,abst->abpt", placing, picked, precision=highest)
-    gathered = lax.all_gather(compact, ("row", "col"), axis=2, tiled=True)
+    gathered = jnp.concatenate(
+        lax.all_to_all(jnp.stack([compact] * lax.axis_size(("row", "col"))), ("row", "col"), 0, 0),
+        axis=2,
+    )
     wanted = my_index * slots_here + jnp.arange(slots_here, dtype=jnp.int32)
     source = holder[wanted] * hold_slots + position[wanted]
     mine = jnp.take(gathered, source, axis=2)

time: 280 us -> 292 us (1.043)
  between operations: 15.6 us -> 2.38 us
  local copies, waits for them, and re-layouts: 39.7 us -> 51.6 us
  starting transfers between devices: 14.4 us -> 26 us
    all_to_all x0 -> x1, waiting for transfers between devices: none -> 71.6 us  [local(): lax.all_to_all(jnp.stack([compact] * lax.axis_size(('row', 'col'))), ('ro...]
    all_gather x1 -> x0, waiting for transfers between devices: 69.5 us -> none  [local(): gathered = lax.all_gather(compact, ('row', 'col'), axis=2, tiled=True)]
    all_to_all x0 -> x1, starting transfers between devices: none -> 11.6 us  [local(): lax.all_to_all(jnp.stack([compact] * lax.axis_size(('row', 'col'))), ('ro...]
    all_gather x1 -> x0, local copies, waits for them, and re-layouts: 10.5 us -> none  [local(): gathered = lax.all_gather(compact, ('row', 'col'), axis=2, tiled=True)]
    reshape x0 -> x1, local copies, waits for them, and re-layouts: none -> 10.3 us  [local(): jnp.concatenate(lax.all_to_all(jnp.stack([compact] * lax.axis_size(('row'...]
    all_to_all x0 -> x1, local copies, waits for them, and re-layouts: none -> 5.89 us  [local(): lax.all_to_all(jnp.stack([compact] * lax.axis_size(('row', 'col'))), ('ro...]
    another operation x0 -> x1, local copies, waits for them, and re-layouts: none -> 3.51 us  [local(): jnp.stack([compact] * lax.axis_size(('row', 'col')))]
  transfers between devices with their start and end apart: 3 -> 3, of which waited for: 2 -> 2; matrix products, arithmetic and copies ran while one was open for 14% -> 13% of each run, Pallas kernels for 0% -> 0%
where the time goes in v1:
time: 292 us; the launch traced here: 288 us
  waiting for transfers between devices  105 us (36%)
  matrix products  70.2 us (24%)
  local copies, waits for them, and re-layouts  51.6 us (18%)
  other arithmetic  32.8 us (11%)
  starting transfers between devices  26 us (9%)
    all_to_all x1, waiting for transfers between devices, local(): lax.all_to_all(jnp.stack([compact] * lax.axis_size(('row', 'col'))), ('ro...  71.6 us
    all_to_all x1, waiting for transfers between devices, sent_together(): lax.all_to_all(both, axis, split_axis=split_dim, concat_axis=concat_dim,...  33.6 us
    dot_general x2, matrix products, circle_forcing(): lax.dot_general(synth_table, columns, (((0,), (0,)), ((), ())), precision...  22 us
    dot_general x2, matrix products, circle_forcing(): return jnp.dot(anal_table, squared, precision=highest).reshape(moved.shape)  20.2 us
    mul x1, other arithmetic, circle_tables(): anal_table = jnp.concatenate([keeping * cosine, -keeping * sine], axis=0)  14.3 us
    mul x1, other arithmetic, circle_tables(): synth_table = jnp.concatenate([weight * cosine, -weight * sine], axis=0)  14.2 us
    dot_general x1, matrix products, spectral_update(): jnp.einsum('fckr,fkq->fcrq', left, right, precision=highest)  14 us
    all_to_all x1, starting transfers between devices, local(): lax.all_to_all(jnp.stack([compact] * lax.axis_size(('row', 'col'))), ('ro...  11.6 us
  transfers between devices with their start and end apart: 3, of which 2 were waited for; matrix products, arithmetic and copies ran while one was open for 13% of the time, Pallas kernels for 0%

profile of v1, /device:TPU:1, one launch (start us, length us, event | category | flops | bytes accessed | tf_op | source)
XLA Modules:
  0.0 288.4 jit_solution(9926440531719303541)
XLA Ops:
  0.6 0.0 copy-start
  0.6 0.0 copy-start.10
  0.7 3.1 %copy.50 = f32[2,32,16,384]{3,1,0,2:T(8,128)} copy(f32[2,32,16,384]{3,2,1,0:T(8,128)} %param.10) | data formatting | bytes 3145728 | tf_op args[0]
  3.8 7.6 %all-to-all-start = ((f32[2,32,16,384]{3,1,0,2:T(8,128)}), f32[2,32,16,384]{3,1,0,2:T(8,128)S(1)}, u32[]{:S(2)}, u32[]{:S(2)}) async-start(f32[2,32,16,384]{3,1,0,2:T(8,128)} %copy.50), calls=%async_computation | async-start | bytes 3145728 | tf_op jit(solution)/shard_map/all_to_all | solution.py:120
  11.4 0.0 copy-done.10
  11.4 0.2 add_divide_fusion
  11.6 14.2 %fusion.12 = (f32[512,1536]{1,0:T(8,128)}, f32[512,1536]{1,0:T(8,128)}) fusion(f32[512]{0:T(512)S(1)} %select_multiply_fusion, f32[512]{0:T(512)S(1)} %fusion.55), kind=kLoop, calls=%fused_computation.28 | loop fusion | flops 8650752 | bytes 6295552 | tf_op jit(solution)/shard_map/mul | solution.py:36
  25.8 14.3 %fusion.13 = (f32[512,1536]{1,0:T(8,128)}, f32[512,1536]{1,0:T(8,128)}) fusion(f32[512]{0:T(512)S(1)} %fusion.43, f32[512]{0:T(512)S(1)} %fusion.54), kind=kLoop, calls=%fused_computation.29 | loop fusion | flops 8650752 | bytes 6295552 | tf_op jit(solution)/shard_map/mul | solution.py:37
  40.2 0.0 all-to-all-done
  40.2 0.0 copy-start.6
  40.2 0.1 copy.51
  40.3 1.8 copy-done.6
  42.1 0.0 copy-start.3
  42.1 0.0 copy-start.4
  42.1 12.0 %fusion.4 = f32[1536,384]{1,0:T(8,128)S(1)} fusion(f32[1024,384]{1,0:T(8,128)S(1)} %bitcast.90, f32[512,1536]{1,0:T(8,128)} %get-tuple-element.48, f32[512,1536]{1,0:T(8,128)S(1)} %copy-done.6), kind=kOutput, calls=%fused_computation.16 | convolution fusion | flops 7249920000 | bytes 10223616 | tf_op jit(solution)/shard_map/dot_general | solution.py:43
  54.1 0.0 copy-done.3
  54.1 0.0 copy-done.4
  54.1 10.1 %multiply_subtract_fusion.1 = f32[1024,384]{1,0:T(8,128)S(1)} fusion(f32[1024,384]{1,0:T(8,128)S(1)} %bitcast.91, f32[1536,384]{1,0:T(8,128)S(1)} %fusion.4, f32[512,1536]{1,0:T(8,128)S(1)} %copy-done.4, f32[512,1536]{1,0:T(8,128)S(1)} %copy-done.3), kind=kOutput, calls=%fused_computation.39 | convolution fusion | flops 7250116608 | bytes 11796480 | tf_op jit(solution)/shard_map/dot_general | solution.py:45
  64.3 0.0 copy-start.8
  64.3 0.0 copy-done
  64.3 0.0 copy-start.7
  64.3 3.2 %convolution_multiply_fusion = f32[2,512,384]{2,1,0:T(8,128)S(1)} fusion(f32[2,512,384]{2,1,0:T(8,128)S(1)} %bitcast.92, f32[512,384]{1,0:T(8,128)S(1)} %add_divide_fusion, f32[384,384]{1,0:T(8,128)S(1)} %copy-done), kind=kOutput, calls=%fused_computation.41 | convolution fusion | flops 1812332544 | bytes 4521984 | tf_op jit(solution)/shard_map/dot_general | solution.py:61
  67.5 0.0 copy-done.8
  67.5 3.4 %fusion.77 = f32[1024,384]{1,0:T(8,128)S(1)} fusion(f32[1024,384]{1,0:T(8,128)S(1)} %bitcast.88, f32[384,384]{1,0:T(8,128)S(1)} %copy-done.8), kind=kOutput, calls=%fused_computation.150 | convolution fusion | flops 1811939328 | bytes 3735552 | tf_op jit(solution)/shard_map/dot_general | solution.py:64
  71.0 0.0 copy-done.7
  71.0 10.0 %fusion.5 = f32[1536,384]{1,0:T(8,128)S(1)} fusion(f32[1024,384]{1,0:T(8,128)S(1)} %fusion.77, f32[512,1536]{1,0:T(8,128)S(1)} %copy-done.7, f32[512,1536]{1,0:T(8,128)S(1)} %copy-done.6), kind=kOutput, calls=%fused_computation.17 | convolution fusion | flops 7249920000 | bytes 10223616 | tf_op jit(solution)/shard_map/dot_general | solution.py:43
  81.0 10.1 %multiply_subtract_fusion = f32[1024,384]{1,0:T(8,128)S(1)} fusion(f32[1024,384]{1,0:T(8,128)S(1)} %fusion.77, f32[1536,384]{1,0:T(8,128)S(1)} %fusion.5, f32[512,1536]{1,0:T(8,128)S(1)} %copy-done.4, f32[512,1536]{1,0:T(8,128)S(1)} %copy-done.3), kind=kOutput, calls=%fused_computation.38 | convolution fusion | flops 7250116608 | bytes 11796480 | tf_op jit(solution)/shard_map/dot_general | solution.py:45
  91.1 3.2 %fusion.29 = f32[2,512,384]{2,1,0:T(8,128)S(1)} fusion(f32[2,512,384]{2,1,0:T(8,128)S(1)} %bitcast.89, f32[384,384]{1,0:T(8,128)S(1)} %copy-done), kind=kOutput, calls=%fused_computation.48 | convolution fusion | flops 1811939328 | bytes 3735552 | tf_op jit(solution)/shard_map/dot_general | solution.py:61
  94.3 3.3 %fusion.21 = f32[2,512,1,384]{3,1,0,2:T(8,128)S(1)} fusion(f32[2,512,384]{2,1,0:T(8,128)S(1)} %fusion.29, f32[512,384]{1,0:T(8,128)S(1)} %add_divide_fusion, f32[384,384]{1,0:T(8,128)S(1)} %copy-done.8), kind=kOutput, calls=%fused_computation.40 | convolution fusion | flops 1812332544 | bytes 4521984 | tf_op jit(solution)/shard_map/dot_general | solution.py:64
  97.5 0.2 pad_maximum_fusion.10
  97.7 3.7 %copy.52 = f32[4,512,1,384]{3,0,2,1:T(4,128)} copy(f32[4,512,1,384]{3,1,0,2:T(8,128)S(1)} %pad_maximum_fusion.10) | data formatting | bytes 6291456 | tf_op jit(solution)/shard_map/concatenate | solution.py:16
  101.4 6.8 %all-to-all-start.1 = ((f32[4,512,1,384]{3,0,2,1:T(4,128)}), f32[4,512,1,384]{3,0,2,1:T(4,128)}, u32[]{:S(2)}, u32[]{:S(2)}) async-start(f32[4,512,1,384]{3,0,2,1:T(4,128)} %copy.52), calls=%async_computation.1 | async-start | bytes 6291456 | tf_op jit(solution)/shard_map/all_to_all | solution.py:18
  108.3 0.0 copy-done.11
  108.3 1.4 scatter_custom_fusion
  109.7 0.0 copy-done.2
  109.7 2.5 gather_fusion.1
  112.2 2.5 gather_fusion
  114.7 0.2 select_reduce_fusion
  114.9 33.6 %all-to-all-done.1 = f32[4,512,1,384]{3,0,2,1:T(4,128)} async-done(((f32[4,512,1,384]{3,0,2,1:T(4,128)}), f32[4,512,1,384]{3,0,2,1:T(4,128)}, u32[]{:S(2)}, u32[]{:S(2)}) %all-to-all-start.1) | async-done | bytes 3145760 | tf_op jit(solution)/shard_map/all_to_all | solution.py:18
  148.5 2.8 copy.90
  151.3 2.9 %slice_bitcast_fusion = (f32[1,2,32,16,384]{4,1,3,2,0:T(2,128)S(1)}, f32[1,2,32,16,384]{4,1,3,2,0:T(2,128)S(1)}, f32[2,32,16,384]{3,0,2,1:T(2,128)}) fusion(f32[4,32,16,1,384]{4,0,2,1,3:T(4,128)S(1)} %bitcast.85), kind=kLoop, calls=%fused_computation.33 | loop fusion | bytes 7864320 | tf_op jit(solution)/shard_map/stack | solution.py:138
  154.2 3.3 %pad_maximum_fusion.11 = f32[2,2,32,16,384]{4,1,3,2,0:T(2,128)} fusion(f32[1,2,32,16,384]{4,1,3,2,0:T(2,128)S(1)} %get-tuple-element.27, f32[1,2,32,16,384]{4,1,3,2,0:T(2,128)S(1)} %get-tuple-element.26), kind=kLoop, calls=%fused_computation.21 | loop fusion | flops 786432 | bytes 6291456 | tf_op jit(solution)/shard_map/stack | solution.py:138
  157.5 4.7 %gather_fusion.4 = f32[256,2,2,384]{3,2,1,0:T(2,128)S(1)} fusion(f32[2,2,32,16,384]{4,1,3,2,0:T(2,128)} %pad_maximum_fusion.11, s32[256]{0:T(256)S(1)} %bitcast.83), kind=kCustom, calls=%fused_computation.4 | custom fusion | bytes 3147776 | tf_op jit(solution)/shard_map/gather | solution.py:139
  162.2 0.9 fusion.24
  163.1 3.5 %stack.26 = f32[128,2,2,8,384]{4,3,2,1,0:T(8,128)} broadcast(f32[2,2,8,384]{3,2,1,0:T(8,128)S(1)} %fusion.24), dimensions={1,2,3,4} | broadcast | bytes 6340608 | tf_op jit(solution)/shard_map/stack | solution.py:154
  166.6 11.6 %all-to-all-start.2 = ((f32[128,2,2,8,384]{4,3,2,1,0:T(8,128)}), f32[128,2,2,8,384]{4,3,2,1,0:T(8,128)}, u32[]{:S(2)}, u32[]{:S(2)}) async-start(f32[128,2,2,8,384]{4,3,2,1,0:T(8,128)} %stack.26), calls=%async_computation.2 | async-start | bytes 12582912 | tf_op jit(solution)/shard_map/all_to_all | solution.py:154
  178.2 0.6 gather_fusion.3
  178.9 0.6 gather_fusion.2
  180.3 0.0 copy-done.9
  180.4 0.0 copy-done.12
  180.4 0.1 cosine_multiply_fusion.1
  180.5 0.1 sine_multiply_fusion
  180.5 0.0 copy-done.5
  180.5 1.3 copy.63
  181.8 71.6 %all-to-all-done.2 = f32[128,2,2,8,384]{4,3,2,1,0:T(8,128)} async-done(((f32[128,2,2,8,384]{4,3,2,1,0:T(8,128)}), f32[128,2,2,8,384]{4,3,2,1,0:T(8,128)}, u32[]{:S(2)}, u32[]{:S(2)}) %all-to-all-start.2) | async-done | bytes 6291488 | tf_op jit(solution)/shard_map/all_to_all | solution.py:154
  253.4 5.9 %copy.89 = f32[128,2,2,8,384]{4,3,0,2,1:T(8,128)} copy(f32[128,2,2,8,384]{4,3,2,1,0:T(8,128)} %all-to-all-done.2) | data formatting | bytes 12582912 | tf_op jit(solution)/shard_map/all_to_all | solution.py:154
  259.3 10.3 %copy.58 = f32[2,2,1024,384]{3,1,2,0:T(2,128)} copy(f32[2,2,1024,384]{3,2,1,0:T(8,128)} %bitcast.82) | data formatting | bytes 12582912 | tf_op jit(solution)/shard_map/reshape | solution.py:153
  269.6 3.4 %gather_fusion.5 = f32[2,2,2,384]{3,2,1,0:T(2,128)S(1)} fusion(f32[2,2,1024,384]{3,1,2,0:T(2,128)} %copy.58, s32[1024]{0:T(1024)S(1)} %pad_clamp_fusion), kind=kCustom, calls=%fused_computation.5 | custom fusion | bytes 24584 | tf_op jit(solution)/shard_map/jit(_take)/gather | solution.py:159
  273.0 0.1 select_bitcast_fusion
  273.1 0.1 slice_negate_fusion.1
  273.2 0.6 copy.64
  273.9 0.0 copy-start.1
  273.9 14.0 %convolution_add_fusion = f32[2,4,2,384,384]{4,3,2,1,0:T(8,128)} fusion(f32[2,4,2,384,384]{4,3,2,1,0:T(8,128)} %param.19, f32[2,4,2,4,384]{4,1,3,0,2:T(4,128)S(1)} %pad_maximum_fusion.16, f32[2,4,4,384,1]{3,1,2,0,4:T(4,128)S(1)} %get-tuple-element.30), kind=kOutput, calls=%fused_computation.15 | convolution fusion | flops 115605504 | bytes 19021824 | tf_op jit(solution)/shard_map/vmap(fckr,fkq->fcrq)/dot_general | solution.py:95
  287.9 0.0 copy-done.1
  (29 shorter events, 0.2 us)
Async XLA Ops:
  0.6 63.7 %copy-start = (f32[384,384]{1,0:T(8,128)S(1)}, f32[384,384]{1,0:T(8,128)}, u32[]{:S(2)}) copy-start(f32[384,384]{1,0:T(8,128)} %param.12) | copy-start | bytes 1769476
  0.6 10.8 %copy-start.10 = (f32[384]{0:T(512)S(1)}, f32[384]{0:T(512)}, u32[]{:S(2)}) copy-start(f32[384]{0:T(512)} %param.13) | copy-start | bytes 4612
  3.8 36.4 %all-to-all-start = ((f32[2,32,16,384]{3,1,0,2:T(8,128)}), f32[2,32,16,384]{3,1,0,2:T(8,128)S(1)}, u32[]{:S(2)}, u32[]{:S(2)}) async-start(f32[2,32,16,384]{3,1,0,2:T(8,128)} %copy.50), calls=%async_computation | async-start | bytes 3145728 | tf_op jit(solution)/shard_map/all_to_all | solution.py:120
  40.2 1.9 copy-start.6
  42.1 12.0 %copy-start.3 = (f32[512,1536]{1,0:T(8,128)S(1)}, f32[512,1536]{1,0:T(8,128)}, u32[]{:S(2)}) copy-start(f32[512,1536]{1,0:T(8,128)} %get-tuple-element.49) | copy-start | bytes 9437188
  42.1 12.0 %copy-start.4 = (f32[512,1536]{1,0:T(8,128)S(1)}, f32[512,1536]{1,0:T(8,128)}, u32[]{:S(2)}) copy-start(f32[512,1536]{1,0:T(8,128)} %get-tuple-element.50) | copy-start | bytes 9437188
  64.3 3.2 %copy-start.8 = (f32[384,384]{1,0:T(8,128)S(1)}, f32[384,384]{1,0:T(8,128)}, u32[]{:S(2)}) copy-start(f32[384,384]{1,0:T(8,128)} %param.11) | copy-start | bytes 1769476
  64.3 6.7 %copy-start.7 = (f32[512,1536]{1,0:T(8,128)S(1)}, f32[512,1536]{1,0:T(8,128)}, u32[]{:S(2)}) copy-start(f32[512,1536]{1,0:T(8,128)} %get-tuple-element.48) | copy-start | bytes 9437188
  101.4 6.8 %copy-start.11 = (s32[256]{0:T(256)S(1)}, s32[256]{0:T(256)}, u32[]{:S(2)}) copy-start(s32[256]{0:T(256)} %param.15) | copy-start | bytes 3076
  101.4 8.3 %copy-start.2 = (s32[256,2]{0,1:T(2,128)S(1)}, s32[256,2]{0,1:T(2,128)}, u32[]{:S(2)}) copy-start(s32[256,2]{0,1:T(2,128)} %param.14) | copy-start | bytes 6148
  101.4 47.1 %all-to-all-start.1 = ((f32[4,512,1,384]{3,0,2,1:T(4,128)}), f32[4,512,1,384]{3,0,2,1:T(4,128)}, u32[]{:S(2)}, u32[]{:S(2)}) async-start(f32[4,512,1,384]{3,0,2,1:T(4,128)} %copy.52), calls=%async_computation.1 | async-start | bytes 6291456 | tf_op jit(solution)/shard_map/all_to_all | solution.py:18
  166.6 13.7 %copy-start.9 = (f32[2,4,2,384]{3,2,1,0:T(2,128)S(1)}, f32[2,4,2,384]{3,2,1,0:T(2,128)}, u32[]{:S(2)}) copy-start(f32[2,4,2,384]{3,2,1,0:T(2,128)} %param.18) | copy-start | bytes 73732
  166.6 13.8 %copy-start.12 = (s32[4]{0:T(128)S(1)}, s32[4]{0:T(128)}, u32[]{:S(2)}) copy-start(s32[4]{0:T(128)} %param.16) | copy-start | bytes 52
  166.6 13.9 %copy-start.5 = (f32[2,32,16,384]{3,0,2,1:T(2,128)S(1)}, f32[2,32,16,384]{3,0,2,1:T(2,128)}, u32[]{:S(2)}) copy-start(f32[2,32,16,384]{3,0,2,1:T(2,128)} %get-tuple-element.28) | copy-start | bytes 4718596
  166.6 86.9 %all-to-all-start.2 = ((f32[128,2,2,8,384]{4,3,2,1,0:T(8,128)}), f32[128,2,2,8,384]{4,3,2,1,0:T(8,128)}, u32[]{:S(2)}, u32[]{:S(2)}) async-start(f32[128,2,2,8,384]{4,3,2,1,0:T(8,128)} %stack.26), calls=%async_computation.2 | async-start | bytes 12582912 | tf_op jit(solution)/shard_map/all_to_all | solution.py:154
  273.9 14.0 %copy-start.1 = (f32[384,384]{1,0:T(8,128)S(1)}, f32[384,384]{1,0:T(8,128)}, u32[]{:S(2)}) copy-start(f32[384,384]{1,0:T(8,128)} %param.12) | copy-start | bytes 1769476
